TPU v7x, 32 devices: a whole 2x2x4 slice. The times are simulated.
32 devices in a mesh: wide: 16 (over z, x, core), narrow: 2 (over y).
Axes of the slice: x: 2, y: 2, z: 4, core: 2. Of those that a mesh axis runs over, the one named last changes fastest.
Arguments:
- hidden: bfloat16 [128, 16384], P('wide', 'narrow'), may hold values from -6 to 6
- down_weight: bfloat16 [16384, 4096], P(('wide', 'narrow')), may hold values from -0.046875 to 0.046875
- rotation: float32 [4096, 4096], P('wide', 'narrow'), may hold values from -1 to 1, as said below
- cotangent: bfloat16 [128, 4096], P('wide', 'narrow'), may hold values from -6 to 6
- token_exps: int32 [128], P('wide'), may hold values from -2 to 0
- column_exps: int32 [4096], P('narrow'), may hold values from -9 to -7
- sign_bits: int32 [16384], P('narrow'), may hold values 0 or 1
- step_size: float32 [], replicated, may hold values from 0.00015 to 0.0003
Outputs:
- projected: bfloat16 [128, 4096], P('wide', 'narrow')
- new_rotation: float32 [4096, 4096], P('wide', 'narrow')
Inputs may be any that keep to these rules, and one draw needn't show every extreme that they name: `rotation`: an orthogonal matrix up to float32 rounding.
All inputs are finite; a program needn't handle non-finite values. No bound on the sum of `sign_bits` on one device may be relied on, other than what follows from the above.
Results may differ from a plain program's by a relative error of at most 0.003.
The roundings to bfloat16 on the way count: a program that leaves them out, or rounds other values in their place, can miss the bound.
Values may be sent and summed in bfloat16 or wider, within the bound.
No kernel may reach another device: no remote copies, remote signals or barrier semaphores. Data moves between devices by JAX's collectives and lax.ppermute only.
A program may use at most 128 MiB of HBM per device.

v0:
```python
import math
import jax
import jax.numpy as jnp
from jax import lax
from jax.sharding import PartitionSpec as P

D = 4096
FF = 16384
HIGHEST_PREC = lax.Precision.HIGHEST
LEVELS = 7.0
TWO_PI = 2.0 * math.pi


def sylvester(length):
    positions = jnp.arange(length, dtype=jnp.int32)
    common = jnp.bitwise_and(positions[:, None], positions[None, :])
    parity = jnp.zeros((length, length), jnp.int32)
    for offset in range(max(length.bit_length() - 1, 0)):
        parity = parity + jnp.bitwise_and(jnp.right_shift(common, offset), 1)
    return (1 - 2 * (parity % 2)).astype(jnp.float32)


def local_hadamard(values):
    row_count, length = values.shape
    inner_size = min(length, 128)
    outer_size = length // inner_size
    blocks = values.reshape(row_count, outer_size, inner_size)
    blocks = jnp.einsum("rab,bc->rac", blocks, sylvester(inner_size), precision=HIGHEST_PREC)
    blocks = jnp.einsum("rab,ac->rcb", blocks, sylvester(outer_size), precision=HIGHEST_PREC)
    return blocks.reshape(row_count, length)


def fake_quant(values, exponents):
    scales = jnp.exp2(exponents.astype(jnp.float32))
    clipped = LEVELS * jnp.tanh(values / scales / LEVELS)
    return scales * (clipped - jnp.sin(TWO_PI * clipped) / TWO_PI)


def inner_rows(left, right):
    return lax.dot_general(left, right, (((0,), (0,)), ((), ())), precision=HIGHEST_PREC)


def on_device(
    hidden, down_weight, rotation, cotangent, token_exps, column_exps, sign_bits, step_size
):
    narrow_count = lax.axis_size("narrow")
    sign_flip = (1 - 2 * sign_bits).astype(jnp.float32)
    partial_mix = local_hadamard(hidden.astype(jnp.float32) * sign_flip[None, :])
    joined = lax.all_gather(partial_mix, "narrow", axis=1, tiled=True)
    row_count = joined.shape[0]
    stacked = joined.reshape(row_count, narrow_count, -1)
    stacked = jnp.einsum("rnf,nm->rmf", stacked, sylvester(narrow_count), precision=HIGHEST_PREC)
    rotated = stacked.reshape(row_count, -1) / math.sqrt(FF)
    token_block = fake_quant(rotated, token_exps[:, None]).astype(jnp.bfloat16)
    quantized = lax.all_to_all(token_block, "wide", split_axis=1, concat_axis=0, tiled=True)
    weight_panel = lax.all_gather(down_weight, "narrow", axis=0, tiled=True)
    rot_half = rotation.astype(jnp.bfloat16)
    col_width = rotation.shape[1]
    weight_rot = jnp.dot(
        weight_panel,
        lax.all_gather(rot_half, "wide", axis=0, tiled=True),
        preferred_element_type=jnp.float32,
    )
    weight_quant = fake_quant(weight_rot, column_exps[None, :]).astype(jnp.bfloat16)
    col_start = lax.axis_index("narrow") * col_width
    weight_local = lax.dynamic_slice_in_dim(weight_panel, col_start, col_width, 1)
    both_weights = jnp.concatenate([weight_quant, weight_local], axis=1)
    summed = lax.psum_scatter(
        jnp.dot(quantized, both_weights, preferred_element_type=jnp.float32),
        "wide",
        scatter_dimension=0,
        tiled=True,
    )
    projected = summed[:, :col_width].astype(jnp.bfloat16)
    unrotated = summed[:, col_width:].astype(jnp.bfloat16)
    target_rows = lax.all_gather(cotangent, "wide", axis=0, tiled=True)
    mixed_wide = lax.all_gather(unrotated, "narrow", axis=1, tiled=True)
    mixed_cols = lax.all_to_all(mixed_wide, "wide", split_axis=1, concat_axis=0, tiled=True)
    gradient = lax.dot_general(
        mixed_cols, target_rows, (((0,), (0,)), ((), ())), preferred_element_type=jnp.float32
    )
    target_wide = target_rows.astype(jnp.float32)
    part_proj = jnp.dot(target_wide, rotation.T, precision=HIGHEST_PREC)
    projection = lax.psum(part_proj.astype(jnp.bfloat16), "narrow").astype(jnp.float32)
    factors = jnp.concatenate([mixed_cols.astype(jnp.float32), projection], axis=0)
    token_count = mixed_cols.shape[0]
    current = rotation - step_size * gradient
    applied = lax.psum(jnp.dot(factors, rotation + current, precision=HIGHEST_PREC), "wide")
    turned = inner_rows(factors[:token_count], applied[token_count:]) - inner_rows(
        factors[token_count:], applied[:token_count]
    )
    current = rotation - 0.5 * step_size * turned
    return (projected, math.sqrt(D) * current)


def solution(mesh):
    in_specs = (
        P("wide", "narrow"),
        P(("wide", "narrow"), None),
        P("wide", "narrow"),
        P("wide", "narrow"),
        P("wide"),
        P("narrow"),
        P("narrow"),
        P(),
    )
    out_specs = (P("wide", "narrow"), P("wide", "narrow"))
    return jax.shard_map(
        on_device, mesh=mesh, in_specs=in_specs, out_specs=out_specs, check_vma=False
    )
```

profile of v0, /device:TPU:0, one launch (start us, length us, event | category | flops | bytes accessed | tf_op | source)
XLA Modules:
  0.0 513.1 jit_solution(12951212293462382946)
XLA Ops:
  7.2 0.7 all-gather.3.cloned.1.call-update
  8.0 0.8 copy-done
  8.8 1.1 convert_element_type.49
  10.0 0.4 fusion.14
  10.4 0.4 convolution_bitcast_fusion
  11.0 10.0 %all_gather.15 = f32[8,16384]{1,0:T(8,128)S(1)} all-gather(f32[8,8192]{1,0:T(8,128)S(1)} %bitcast.42), channel_id=1, replica_groups=mesh['wide'=16,'narrow'=2] {'narrow'}, dimensions={1}, use_global_device_ids=true | all-gather | bytes 786432 | tf_op jit(solution)/shard_map/all_gather | solution.py:49
  20.9 0.5 reshape.43
  21.4 2.7 fusion
  24.1 1.6 div.38
  25.7 2.8 multiply_convert_fusion.1
  28.5 6.1 %all-to-all-start = ((bf16[8,16,1024]{2,0,1:T(8,128)(2,1)}), bf16[8,16,1024]{2,0,1:T(8,128)(2,1)S(1)}, u32[]{:S(2)}, u32[]{:S(2)}) async-start(bf16[8,16,1024]{2,0,1:T(8,128)(2,1)} %multiply_convert_fusion.1), calls=%async_computation | async-start | bytes 524288 | tf_op jit(solution)/shard_map/all_to_all | solution.py:55
  34.6 0.2 reduce-scatter.2.cloned.1.call-start
  34.9 81.4 %all-gather.3.cloned.1.call-done = bf16[1024,4096]{1,0:T(8,128)(2,1)} async-done(((bf16[512,4096]{1,0:T(8,128)(2,1)}), bf16[1024,4096]{1,0:T(8,128)(2,1)}) %all-gather.3.cloned.1.call-update) | async-done | bytes 8388624 | tf_op jit(solution)/shard_map/all_gather | solution.py:56
  116.3 4.7 constant_dynamic-slice_fusion
  121.0 124.5 %all-gather.5.cloned.1.call-done = bf16[4096,2048]{1,0:T(8,128)(2,1)} async-done(((bf16[256,2048]{1,0:T(8,128)(2,1)}), bf16[4096,2048]{1,0:T(8,128)(2,1)}) %all-gather.5.cloned.1.call-update) | async-done | bytes 16777232 | tf_op jit(solution)/shard_map/all_gather | solution.py:61
  245.5 51.8 %multiply_convert_fusion = bf16[1024,2048]{1,0:T(8,128)(2,1)} fusion(bf16[1024,4096]{1,0:T(8,128)(2,1)} %all-gather.3.cloned.1.call-done, bf16[4096,2048]{1,0:T(8,128)(2,1)} %all-gather.5.cloned.1.call-done, f32[2048]{0:T(1024)S(1)} %multiply_exponential_fusion), kind=kOutput, calls=%fused_computation.6 | convolution fusion | flops 17196646400 | bytes 29368320 | tf_op jit(solution)/shard_map/dot_general | solution.py:59
  297.2 5.5 %fusion.1 = f32[128,4096]{1,0:T(8,128)} fusion(bf16[1024,2048]{1,0:T(8,128)(2,1)} %constant_dynamic-slice_fusion, bf16[1024,2048]{1,0:T(8,128)(2,1)} %multiply_convert_fusion, bf16[8,16,1024]{2,0,1:T(8,128)(2,1)S(1)} %all-to-all-done), kind=kOutput, calls=%fused_computation.2 | convolution fusion | flops 1090519040 | bytes 10747904 | tf_op jit(solution)/shard_map/dot_general | solution.py:69
  302.8 19.9 %all_gather.19 = bf16[128,2048]{1,0:T(8,128)(2,1)S(1)} all-gather(bf16[8,2048]{1,0:T(8,128)(2,1)S(1)} %copy-done.3), channel_id=1, replica_groups=mesh['wide'=16,'narrow'=2] {'wide'}, dimensions={0}, use_global_device_ids=true | all-gather | bytes 557056 | tf_op jit(solution)/shard_map/all_gather | solution.py:76
  322.7 40.3 %reduce-scatter.2.cloned.1.call-done = f32[8,4096]{1,0:T(8,128)} async-done(((f32[128,4096]{1,0:T(8,128)}), f32[8,4096]{1,0:T(8,128)}) %reduce-scatter.2.cloned.1.call-update) | async-done | bytes 131088 | tf_op jit(solution)/shard_map/reduce_scatter | solution.py:68
  362.9 0.9 convert.5
  363.9 0.6 fusion.85
  364.5 4.7 all_gather.18
  369.2 3.7 all-to-all-start.1
  372.8 0.3 all-reduce.3.cloned.1.call-start
  373.1 1.9 convolution_convert_fusion
  375.7 4.0 all-to-all-done.1
  379.7 1.8 subtract_add_fusion
  381.5 16.3 %all-reduce.3.cloned.1.call-done = bf16[128,256]{1,0:T(8,128)(2,1)} async-done(((bf16[128,256]{1,0:T(8,128)(2,1)}), bf16[128,256]{1,0:T(8,128)(2,1)}) %all-reduce.3.cloned.1.call-update) | async-done | bytes 65552 | tf_op jit(solution)/shard_map/psum | solution.py:84
  397.8 4.2 fusion.16
  402.0 98.3 %all-reduce.5.cloned.1.call-done = f32[256,2048]{1,0:T(8,128)} async-done(((f32[256,2048]{1,0:T(8,128)}), f32[256,2048]{1,0:T(8,128)}) %all-reduce.5.cloned.1.call-update) | async-done | bytes 2097168 | tf_op jit(solution)/shard_map/psum | solution.py:88
  500.3 2.2 fusion.9
  502.6 3.9 fusion.7
  (26 shorter events, 0.4 us)
Async XLA Ops:
  7.2 1.6 copy-start
  7.2 2.7 copy-start.4
  7.2 2.8 copy-start.2
  7.2 109.1 %all-gather.3.cloned.1.call-start = ((), (), s32[]{:S(2)}) async-start(), calls=%async_computation.3 | async-start | bytes 12582912 | tf_op jit(solution)/shard_map/all_gather | solution.py:56
  7.9 237.5 %all-gather.5.cloned.1.call-start = ((), (), s32[]{:S(2)}) async-start(), calls=%async_computation.4 | async-start | bytes 17825792 | tf_op jit(solution)/shard_map/all_gather | solution.py:61
  9.9 15.8 %copy-start.6 = (s32[8]{0:T(128)S(1)}, s32[8]{0:T(128)}, u32[]{:S(2)}) copy-start(s32[8]{0:T(128)} %param.12) | copy-start | bytes 100
  9.9 25.0 %copy-start.5 = (s32[2048]{0:T(1024)S(1)}, s32[2048]{0:T(1024)}, u32[]{:S(2)}) copy-start(s32[2048]{0:T(1024)} %param.13) | copy-start | bytes 24580
  28.5 268.8 %all-to-all-start = ((bf16[8,16,1024]{2,0,1:T(8,128)(2,1)}), bf16[8,16,1024]{2,0,1:T(8,128)(2,1)S(1)}, u32[]{:S(2)}, u32[]{:S(2)}) async-start(bf16[8,16,1024]{2,0,1:T(8,128)(2,1)} %multiply_convert_fusion.1), calls=%async_computation | async-start | bytes 524288 | tf_op jit(solution)/shard_map/all_to_all | solution.py:55
  34.6 328.3 %reduce-scatter.2.cloned.1.call-start = ((), (), s32[]{:S(2)}) async-start(), calls=%async_computation.5 | async-start | bytes 2228224 | tf_op jit(solution)/shard_map/reduce_scatter | solution.py:68
  297.2 5.6 %copy-start.3 = (bf16[8,2048]{1,0:T(8,128)(2,1)S(1)}, bf16[8,2048]{1,0:T(8,128)(2,1)}, u32[]{:S(2)}) copy-start(bf16[8,2048]{1,0:T(8,128)(2,1)} %param.11) | copy-start | bytes 98308
  369.2 10.6 %all-to-all-start.1 = ((bf16[8,16,256]{2,0,1:T(8,128)(2,1)}), bf16[8,16,256]{2,0,1:T(8,128)(2,1)S(1)}, u32[]{:S(2)}, u32[]{:S(2)}) async-start(bf16[8,16,256]{2,0,1:T(8,128)(2,1)} %bitcast.8), calls=%async_computation.2 | async-start | bytes 131072 | tf_op jit(solution)/shard_map/all_to_all | solution.py:78
  372.8 25.0 %all-reduce.3.cloned.1.call-start = ((), (), s32[]{:S(2)}) async-start(), calls=%async_computation.6 | async-start | bytes 131072 | tf_op jit(solution)/shard_map/psum | solution.py:84
  375.0 125.3 %all-reduce.5.cloned.1.call-start = ((), (), s32[]{:S(2)}) async-start(), calls=%async_computation.7 | async-start | bytes 4194304 | tf_op jit(solution)/shard_map/psum | solution.py:88
  397.8 104.8 %copy-start.1 = (bf16[128,256]{1,0:T(8,128)(2,1)S(1)}, bf16[128,256]{1,0:T(8,128)(2,1)}, u32[]{:S(2)}) copy-start(bf16[128,256]{1,0:T(8,128)(2,1)} %all-reduce.3.cloned.1.call-done) | copy-start | bytes 196612
Sparse Core Ops, SparseCore 0:
  9.5 106.6 all-gather.2
  119.0 126.4 all-gather.4
  302.9 59.9 reduce-scatter.1
  375.6 22.2 all-reduce.2
  402.2 98.1 all-reduce.4
where the time goes:
time: 514 us; the launch traced here: 513 us
  waiting for transfers between devices  365 us (71%)
  matrix products  74.8 us (15%)
  blocking collectives  34.5 us (7%)
  between operations  14.6 us (3%)
  starting transfers between devices  10.4 us (2%)
  local copies, waits for them, and re-layouts  8.37 us (2%)
    all_gather x1, waiting for transfers between devices, on_device(): lax.all_gather(rot_half, 'wide', axis=0, tiled=True)  124 us
    psum x1, waiting for transfers between devices, on_device(): lax.psum(jnp.dot(factors, rotation + current, precision=HIGHEST_PREC), 'w...  98.3 us
    all_gather x1, waiting for transfers between devices, on_device(): weight_panel = lax.all_gather(down_weight, 'narrow', axis=0, tiled=True)  81.4 us
    dot_general x1, matrix products, on_device(): jnp.dot(weight_panel, lax.all_gather(rot_half, 'wide', axis=0, tiled=True...  51.8 us
    reduce_scatter x1, waiting for transfers between devices, on_device(): lax.psum_scatter(jnp.dot(quantized, both_weights, preferred_element_type=...  40.3 us
    all_gather x1, blocking collectives, on_device(): target_rows = lax.all_gather(cotangent, 'wide', axis=0, tiled=True)  19.9 us
    psum x1, waiting for transfers between devices, on_device(): lax.psum(part_proj.astype(jnp.bfloat16), 'narrow').astype(jnp.float32)  16.3 us
  transfers between devices with their start and end apart: 7, of which 6 were waited for; matrix products, arithmetic and copies ran while one was open for 14% of the time, Pallas kernels for 0%

commit v1 on v0

--- a/solution.py
+++ b/solution.py
@@ -85,7 +85,9 @@
     factors = jnp.concatenate([mixed_cols.astype(jnp.float32), projection], axis=0)
     token_count = mixed_cols.shape[0]
     current = rotation - step_size * gradient
-    applied = lax.psum(jnp.dot(factors, rotation + current, precision=HIGHEST_PREC), "wide")
+    applied = jnp.sum(
+        lax.all_gather(jnp.dot(factors, rotation + current, precision=HIGHEST_PREC), "wide"), axis=0
+    )
     turned = inner_rows(factors[:token_count], applied[token_count:]) - inner_rows(
         factors[token_count:], applied[:token_count]
     )

time: 514 us -> 597 us (1.16)
  waiting for transfers between devices: 365 us -> 435 us
  other arithmetic: 4.87 us -> 18 us
    all_gather x0 -> x1, waiting for transfers between devices: none -> 168 us  [on_device(): lax.all_gather(jnp.dot(factors, rotation + current, precision=HIGHEST_PRE...]
    psum x1 -> x0, waiting for transfers between devices: 98.3 us -> none  [on_device(): lax.psum(jnp.dot(factors, rotation + current, precision=HIGHEST_PREC), 'w...]
    reduce_sum x0 -> x1, other arithmetic: none -> 13.1 us  [on_device(): jnp.sum(lax.all_gather(jnp.dot(factors, rotation + current, precision=HIG...]
  transfers between devices with their start and end apart: 7 -> 7, of which waited for: 6 -> 6; matrix products, arithmetic and copies ran while one was open for 14% -> 12% of each run, Pallas kernels for 0% -> 0%
where the time goes in v1:
time: 597 us; the launch traced here: 596 us
  waiting for transfers between devices  435 us (73%)
  matrix products  74.7 us (13%)
  blocking collectives  34.5 us (6%)
  other arithmetic  18 us (3%)
  between operations  14.6 us (2%)
  starting transfers between devices  10.4 us (2%)
  local copies, waits for them, and re-layouts  8.37 us (1%)
    all_gather x1, waiting for transfers between devices, on_device(): lax.all_gather(jnp.dot(factors, rotation + current, precision=HIGHEST_PRE...  168 us
    all_gather x1, waiting for transfers between devices, on_device(): lax.all_gather(rot_half, 'wide', axis=0, tiled=True)  124 us
    all_gather x1, waiting for transfers between devices, on_device(): weight_panel = lax.all_gather(down_weight, 'narrow', axis=0, tiled=True)  81.4 us
    dot_general x1, matrix products, on_device(): jnp.dot(weight_panel, lax.all_gather(rot_half, 'wide', axis=0, tiled=True...  51.8 us
    reduce_scatter x1, waiting for transfers between devices, on_device(): lax.psum_scatter(jnp.dot(quantized, both_weights, preferred_element_type=...  40.3 us
    all_gather x1, blocking collectives, on_device(): target_rows = lax.all_gather(cotangent, 'wide', axis=0, tiled=True)  19.9 us
    psum x1, waiting for transfers between devices, on_device(): lax.psum(part_proj.astype(jnp.bfloat16), 'narrow').astype(jnp.float32)  16.3 us
    reduce_sum x1, other arithmetic, on_device(): jnp.sum(lax.all_gather(jnp.dot(factors, rotation + current, precision=HIG...  13.1 us
  transfers between devices with their start and end apart: 7, of which 6 were waited for; matrix products, arithmetic and copies ran while one was open for 12% of the time, Pallas kernels for 0%

profile of v1, /device:TPU:0, one launch (start us, length us, event | category | flops | bytes accessed | tf_op | source)
XLA Modules:
  0.0 596.0 jit_solution(13270391516895125776)
XLA Ops:
  7.2 0.7 all-gather.5.cloned.1.call-update
  8.0 0.8 copy-done
  8.8 1.1 convert_element_type.49
  10.0 0.4 fusion.14
  10.4 0.4 convolution_bitcast_fusion
  11.0 10.0 %all_gather.21 = f32[8,16384]{1,0:T(8,128)S(1)} all-gather(f32[8,8192]{1,0:T(8,128)S(1)} %bitcast.44), channel_id=1, replica_groups=mesh['wide'=16,'narrow'=2] {'narrow'}, dimensions={1}, use_global_device_ids=true | all-gather | bytes 786432 | tf_op jit(solution)/shard_map/all_gather | solution.py:49
  20.9 0.5 reshape.43
  21.4 2.7 fusion
  24.1 1.6 div.38
  25.7 2.8 multiply_convert_fusion.1
  28.5 6.1 %all-to-all-start = ((bf16[8,16,1024]{2,0,1:T(8,128)(2,1)}), bf16[8,16,1024]{2,0,1:T(8,128)(2,1)S(1)}, u32[]{:S(2)}, u32[]{:S(2)}) async-start(bf16[8,16,1024]{2,0,1:T(8,128)(2,1)} %multiply_convert_fusion.1), calls=%async_computation | async-start | bytes 524288 | tf_op jit(solution)/shard_map/all_to_all | solution.py:55
  34.9 81.4 %all-gather.5.cloned.1.call-done = bf16[1024,4096]{1,0:T(8,128)(2,1)} async-done(((bf16[512,4096]{1,0:T(8,128)(2,1)}), bf16[1024,4096]{1,0:T(8,128)(2,1)}) %all-gather.5.cloned.1.call-update) | async-done | bytes 8388624 | tf_op jit(solution)/shard_map/all_gather | solution.py:56
  116.3 4.7 constant_dynamic-slice_fusion
  121.0 124.5 %all-gather.7.cloned.1.call-done = bf16[4096,2048]{1,0:T(8,128)(2,1)} async-done(((bf16[256,2048]{1,0:T(8,128)(2,1)}), bf16[4096,2048]{1,0:T(8,128)(2,1)}) %all-gather.7.cloned.1.call-update) | async-done | bytes 16777232 | tf_op jit(solution)/shard_map/all_gather | solution.py:61
  245.5 51.8 %multiply_convert_fusion = bf16[1024,2048]{1,0:T(8,128)(2,1)} fusion(bf16[1024,4096]{1,0:T(8,128)(2,1)} %all-gather.5.cloned.1.call-done, bf16[4096,2048]{1,0:T(8,128)(2,1)} %all-gather.7.cloned.1.call-done, f32[2048]{0:T(1024)S(1)} %multiply_exponential_fusion), kind=kOutput, calls=%fused_computation.6 | convolution fusion | flops 17196646400 | bytes 29368320 | tf_op jit(solution)/shard_map/dot_general | solution.py:59
  297.2 5.5 fusion.1
  302.8 19.9 %all_gather.25 = bf16[128,2048]{1,0:T(8,128)(2,1)S(1)} all-gather(bf16[8,2048]{1,0:T(8,128)(2,1)S(1)} %copy-done.3), channel_id=1, replica_groups=mesh['wide'=16,'narrow'=2] {'wide'}, dimensions={0}, use_global_device_ids=true | all-gather | bytes 557056 | tf_op jit(solution)/shard_map/all_gather | solution.py:76
  322.7 40.3 %reduce-scatter.2.cloned.1.call-done = f32[8,4096]{1,0:T(8,128)} async-done(((f32[128,4096]{1,0:T(8,128)}), f32[8,4096]{1,0:T(8,128)}) %reduce-scatter.2.cloned.1.call-update) | async-done | bytes 131088 | tf_op jit(solution)/shard_map/reduce_scatter | solution.py:68
  362.9 0.9 convert.5
  363.9 0.6 fusion.85
  364.5 4.7 all_gather.24
  369.2 3.7 all-to-all-start.1
  372.8 0.3 all-reduce.2.cloned.1.call-start
  373.1 1.9 convolution_convert_fusion
  375.7 4.0 all-to-all-done.1
  379.7 1.8 subtract_add_fusion
  381.5 16.3 %all-reduce.2.cloned.1.call-done = bf16[128,256]{1,0:T(8,128)(2,1)} async-done(((bf16[128,256]{1,0:T(8,128)(2,1)}), bf16[128,256]{1,0:T(8,128)(2,1)}) %all-reduce.2.cloned.1.call-update) | async-done | bytes 65552 | tf_op jit(solution)/shard_map/psum | solution.py:84
  397.8 4.1 fusion.16
  402.0 168.2 %all-gather.9.cloned.1.call-done = f32[4096,2048]{1,0:T(8,128)} async-done(((f32[256,2048]{1,0:T(8,128)}), f32[4096,2048]{1,0:T(8,128)}) %all-gather.9.cloned.1.call-update) | async-done | bytes 33554448 | tf_op jit(solution)/shard_map/all_gather | solution.py:89
  570.2 13.1 %reduce_sum.9 = f32[256,2048]{1,0:T(8,128)} reduce(f32[16,256,2048]{2,1,0:T(8,128)} %bitcast.42, f32[]{:T(128)} %constant.86.clone.1), dimensions={0}, to_apply=%region_2.3 | reduce | flops 7864320 | bytes 35651588 | tf_op jit(solution)/shard_map/reduce_sum | solution.py:88
  583.3 2.2 fusion.9
  585.6 3.9 fusion.7
  (27 shorter events, 0.6 us)
Async XLA Ops:
  7.2 1.6 copy-start
  7.2 2.7 copy-start.4
  7.2 2.8 copy-start.2
  7.2 109.1 %all-gather.5.cloned.1.call-start = ((), (), s32[]{:S(2)}) async-start(), calls=%async_computation.3 | async-start | bytes 12582912 | tf_op jit(solution)/shard_map/all_gather | solution.py:56
  7.9 237.5 %all-gather.7.cloned.1.call-start = ((), (), s32[]{:S(2)}) async-start(), calls=%async_computation.4 | async-start | bytes 17825792 | tf_op jit(solution)/shard_map/all_gather | solution.py:61
  9.9 15.8 %copy-start.6 = (s32[8]{0:T(128)S(1)}, s32[8]{0:T(128)}, u32[]{:S(2)}) copy-start(s32[8]{0:T(128)} %param.12) | copy-start | bytes 100
  9.9 25.0 %copy-start.5 = (s32[2048]{0:T(1024)S(1)}, s32[2048]{0:T(1024)}, u32[]{:S(2)}) copy-start(s32[2048]{0:T(1024)} %param.13) | copy-start | bytes 24580
  28.5 268.8 %all-to-all-start = ((bf16[8,16,1024]{2,0,1:T(8,128)(2,1)}), bf16[8,16,1024]{2,0,1:T(8,128)(2,1)S(1)}, u32[]{:S(2)}, u32[]{:S(2)}) async-start(bf16[8,16,1024]{2,0,1:T(8,128)(2,1)} %multiply_convert_fusion.1), calls=%async_computation | async-start | bytes 524288 | tf_op jit(solution)/shard_map/all_to_all | solution.py:55
  34.6 328.3 %reduce-scatter.2.cloned.1.call-start = ((), (), s32[]{:S(2)}) async-start(), calls=%async_computation.5 | async-start | bytes 2228224 | tf_op jit(solution)/shard_map/reduce_scatter | solution.py:68
  297.2 5.6 copy-start.3
  369.2 10.6 %all-to-all-start.1 = ((bf16[8,16,256]{2,0,1:T(8,128)(2,1)}), bf16[8,16,256]{2,0,1:T(8,128)(2,1)S(1)}, u32[]{:S(2)}, u32[]{:S(2)}) async-start(bf16[8,16,256]{2,0,1:T(8,128)(2,1)} %bitcast.8), calls=%async_computation.2 | async-start | bytes 131072 | tf_op jit(solution)/shard_map/all_to_all | solution.py:78
  372.8 25.0 %all-reduce.2.cloned.1.call-start = ((), (), s32[]{:S(2)}) async-start(), calls=%async_computation.6 | async-start | bytes 131072 | tf_op jit(solution)/shard_map/psum | solution.py:84
  375.0 195.1 %all-gather.9.cloned.1.call-start = ((), (), s32[]{:S(2)}) async-start(), calls=%async_computation.7 | async-start | bytes 35651584 | tf_op jit(solution)/shard_map/all_gather | solution.py:89
  570.2 15.4 %copy-start.1 = (bf16[128,256]{1,0:T(8,128)(2,1)S(1)}, bf16[128,256]{1,0:T(8,128)(2,1)}, u32[]{:S(2)}) copy-start(bf16[128,256]{1,0:T(8,128)(2,1)} %all-reduce.2.cloned.1.call-done) | copy-start | bytes 196612
Sparse Core Ops, SparseCore 0:
  9.5 106.6 all-gather.4
  119.0 126.4 all-gather.6
  302.9 59.9 reduce-scatter.1
  375.6 22.2 all-reduce.1
  402.1 168.0 all-gather.8
